TPU v7x, 32 devices: a whole 2x2x4 slice. The times are simulated.
32 devices in a mesh: shard: 4 (over z), context: 2 (over y), tensor: 4 (over x, core).
Axes of the slice: x: 2, y: 2, z: 4, core: 2. Of those that a mesh axis runs over, the one named last changes fastest.
Arguments:
- tokens: bfloat16 [16, 1024, 1024], P('shard', 'context'), may hold values from -6 to 6
- cotangent: bfloat16 [16, 1024, 1024], P('shard', 'context'), may hold values from -6 to 6
- adapter_index: int32 [16], P('shard'), may hold values from 0 to 7, as said below
- ln1_gain: float32 [1024], replicated, may hold values from 0.5 to 1.5
- ln1_bias: float32 [1024], replicated, may hold values from -1.5 to 1.5
- ln2_gain: float32 [1024], replicated, may hold values from 0.5 to 1.5
- ln2_bias: float32 [1024], replicated, may hold values from -1.5 to 1.5
- layer_scale: float32 [2, 1024], replicated, may hold values from 0.4 to 1.2
- w_qkv: bfloat16 [1024, 3, 1024], P(('shard', 'context'), None, 'tensor'), may hold values from -0.1875 to 0.1875
- w_proj: bfloat16 [1024, 1024], P(('shard', 'context'), 'tensor'), may hold values from -0.5 to 0.5
- w_fc1: bfloat16 [1024, 4096], P(('shard', 'context'), 'tensor'), may hold values from -0.1875 to 0.1875
- w_fc2: bfloat16 [1024, 4096], P(('shard', 'context'), 'tensor'), may hold values from -0.09375 to 0.09375
- down_in: bfloat16 [8, 4, 1024, 16], replicated, may hold values from -0.1875 to 0.1875
- qkv_up: bfloat16 [8, 3, 16, 1024], P(None, None, None, 'tensor'), may hold values from -1.5 to 1.5
- fc1_up: bfloat16 [8, 16, 4096], P(None, None, 'tensor'), may hold values from -1.5 to 1.5
- proj_down: bfloat16 [8, 1024, 16], P(None, 'tensor'), may hold values from -0.5 to 0.5
- fc2_down: bfloat16 [8, 4096, 16], P(None, 'tensor'), may hold values from -0.09375 to 0.09375
- out_up: bfloat16 [8, 2, 16, 1024], replicated, may hold values from -1.5 to 1.5
Outputs:
- result: bfloat16 [16, 1024, 1024], P('shard', 'context')
- input_grad: float32 [16, 1024, 1024], P('shard', 'context')
- down_in_grad: float32 [8, 4, 1024, 16], replicated
- qkv_up_grad: float32 [8, 3, 16, 1024], P(None, None, None, 'tensor')
- fc1_up_grad: float32 [8, 16, 4096], P(None, None, 'tensor')
- proj_down_grad: float32 [8, 1024, 16], P(None, 'tensor')
- fc2_down_grad: float32 [8, 4096, 16], P(None, 'tensor')
- out_up_grad: float32 [8, 2, 16, 1024], replicated
Inputs may be any that keep to these rules, and one draw needn't show every extreme that they name: `adapter_index`: every adapter index is used by exactly 2 images.
All inputs are finite; a program needn't handle non-finite values.
Results may differ from a plain program's by a relative error of at most 0.015.
The roundings to bfloat16 on the way count: a program that leaves them out, or rounds other values in their place, can miss the bound.
Values may be sent and summed in bfloat16 or wider, within the bound.
No kernel may reach another device: no remote copies, remote signals or barrier semaphores. Data moves between devices by JAX's collectives and lax.ppermute only.
A program may use at most 256 MiB of HBM per device.

v0:
```python
import math
import jax
import jax.numpy as jnp
from jax import lax
from jax.sharding import PartitionSpec as P

HEAD_DIM = 64
eps_norm = 1e-06


def normalize(values, norm_gain, norm_shift):
    centre = values - jnp.mean(values, axis=-1, keepdims=True)
    inverse = lax.rsqrt(jnp.mean(centre * centre, axis=-1, keepdims=True) + eps_norm)
    unit_values = centre * inverse
    return (unit_values * norm_gain + norm_shift, unit_values, inverse)


def norm_back(grad_out, unit_values, inverse, norm_gain):
    scaled = grad_out * norm_gain
    centred = scaled - jnp.mean(scaled, axis=-1, keepdims=True)
    return inverse * (
        centred - unit_values * jnp.mean(scaled * unit_values, axis=-1, keepdims=True)
    )


def per_device(
    tokens,
    cotangent,
    adapter_index,
    ln1_gain,
    ln1_bias,
    ln2_gain,
    ln2_bias,
    layer_scale,
    w_qkv,
    w_proj,
    w_fc1,
    w_fc2,
    down_in,
    qkv_up,
    fc1_up,
    proj_down,
    fc2_down,
    out_up,
):
    images, row_count, model_width = tokens.shape
    adapter_count = down_in.shape[0]
    choose = (adapter_index[:, None] == jnp.arange(adapter_count, dtype=jnp.int32)[None, :]).astype(
        jnp.bfloat16
    )
    choose_float = choose.astype(jnp.float32)

    def select_rows(stacked):
        return jnp.einsum(
            "ia,a...->i...", choose, stacked, preferred_element_type=jnp.float32
        ).astype(jnp.bfloat16)

    def collect(per_image):
        return jnp.einsum("ia,i...->a...", choose_float, per_image, precision=lax.Precision.HIGHEST)

    sel_down = select_rows(down_in)
    sel_qkv = select_rows(qkv_up)
    sel_fc1 = select_rows(fc1_up)
    sel_proj = select_rows(proj_down)
    sel_fc2 = select_rows(fc2_down)
    sel_out = select_rows(out_up)
    score_scale = 1.0 / math.sqrt(HEAD_DIM)
    attn_full, proj_full = (
        lax.all_gather(w_qkv, ("shard", "context"), axis=0, tiled=True),
        lax.all_gather(w_proj, ("shard", "context"), axis=0, tiled=True),
    )
    fc1_full, fc2_full = (
        lax.all_gather(w_fc1, ("shard", "context"), axis=0, tiled=True),
        lax.all_gather(w_fc2, ("shard", "context"), axis=0, tiled=True),
    )
    resid = tokens.astype(jnp.float32)
    normed, unit_one, inverse_one = normalize(resid, ln1_gain, ln1_bias)
    normed_low = normed.astype(jnp.bfloat16)
    rank_qkv = jnp.einsum(
        "ild,ikdr->iklr", normed_low, sel_down[:, :3], preferred_element_type=jnp.float32
    ).astype(jnp.bfloat16)
    projected = jnp.einsum(
        "ild,dkc->iklc", normed_low, attn_full, preferred_element_type=jnp.float32
    )
    projected = projected + jnp.einsum(
        "iklr,ikrc->iklc", rank_qkv, sel_qkv, preferred_element_type=jnp.float32
    )
    projected_low = projected.astype(jnp.bfloat16)
    local_width = projected_low.shape[-1]
    head_count = local_width // HEAD_DIM
    queries = projected_low[:, 0].reshape(images, row_count, head_count, HEAD_DIM)
    keys_all, values_all = (
        lax.all_gather(projected_low[:, 1], "context", axis=1, tiled=True),
        lax.all_gather(projected_low[:, 2], "context", axis=1, tiled=True),
    )
    key_heads = keys_all.reshape(images, -1, head_count, HEAD_DIM)
    value_heads = values_all.reshape(images, -1, head_count, HEAD_DIM)
    scores = (
        jnp.einsum("iqhe,ikhe->ihqk", queries, key_heads, preferred_element_type=jnp.float32)
        * score_scale
    )
    row_peak = jnp.max(scores, axis=-1, keepdims=True)
    exp_scores = jnp.exp(scores - row_peak)
    exp_total = jnp.sum(exp_scores, axis=-1, keepdims=True)
    log_total = row_peak + jnp.log(exp_total)
    probabilities = (exp_scores / exp_total).astype(jnp.bfloat16)
    mixed_heads = jnp.einsum(
        "ihqk,ikhe->iqhe", probabilities, value_heads, preferred_element_type=jnp.float32
    )
    mixed_low = mixed_heads.reshape(images, row_count, local_width).astype(jnp.bfloat16)
    proj_part = jnp.einsum("ilc,dc->ild", mixed_low, proj_full, preferred_element_type=jnp.float32)
    proj_rank_part = jnp.einsum(
        "ilc,icr->ilr", mixed_low, sel_proj, preferred_element_type=jnp.float32
    )
    proj_total, proj_rank_total = lax.psum((proj_part, proj_rank_part), "tensor")
    proj_rank = proj_rank_total.astype(jnp.bfloat16)
    attn_out = proj_total + jnp.einsum(
        "ilr,ird->ild", proj_rank, sel_out[:, 0], preferred_element_type=jnp.float32
    )
    hidden_one = resid + layer_scale[0] * attn_out
    normed_two, unit_two, inverse_two = normalize(hidden_one, ln2_gain, ln2_bias)
    normed_two_low = normed_two.astype(jnp.bfloat16)
    fc1_rank = jnp.einsum(
        "ild,idr->ilr", normed_two_low, sel_down[:, 3], preferred_element_type=jnp.float32
    ).astype(jnp.bfloat16)
    preact = jnp.einsum("ild,df->ilf", normed_two_low, fc1_full, preferred_element_type=jnp.float32)
    preact = preact + jnp.einsum(
        "ilr,irf->ilf", fc1_rank, sel_fc1, preferred_element_type=jnp.float32
    )
    activation = jax.nn.gelu(preact, approximate=False).astype(jnp.bfloat16)
    mlp_part = jnp.einsum("ilf,df->ild", activation, fc2_full, preferred_element_type=jnp.float32)
    fc2_rank_part = jnp.einsum(
        "ilf,ifr->ilr", activation, sel_fc2, preferred_element_type=jnp.float32
    )
    mlp_total, fc2_rank_total = (
        lax.psum(mlp_part.astype(jnp.bfloat16), "tensor").astype(jnp.float32),
        lax.psum(fc2_rank_part.astype(jnp.bfloat16), "tensor").astype(jnp.float32),
    )
    fc2_rank = fc2_rank_total.astype(jnp.bfloat16)
    branch = mlp_total + jnp.einsum(
        "ilr,ird->ild", fc2_rank, sel_out[:, 1], preferred_element_type=jnp.float32
    )
    result = (hidden_one + layer_scale[1] * branch).astype(jnp.bfloat16)
    upstream = cotangent.astype(jnp.float32)
    fc1_back, fc2_back = (
        lax.all_gather(w_fc1, ("shard", "context"), axis=0, tiled=True),
        lax.all_gather(w_fc2, ("shard", "context"), axis=0, tiled=True),
    )
    grad_branch = (upstream * layer_scale[1]).astype(jnp.bfloat16)
    grad_fc2_rank = jnp.einsum(
        "ild,ird->ilr", grad_branch, sel_out[:, 1], preferred_element_type=jnp.float32
    ).astype(jnp.bfloat16)
    out_grad_fc2 = jnp.einsum(
        "ilr,ild->ird", fc2_rank, grad_branch, preferred_element_type=jnp.float32
    )
    grad_activation = jnp.einsum(
        "ild,df->ilf", grad_branch, fc2_back, preferred_element_type=jnp.float32
    )
    grad_activation = grad_activation + jnp.einsum(
        "ilr,ifr->ilf", grad_fc2_rank, sel_fc2, preferred_element_type=jnp.float32
    )
    fc2_down_part = jnp.einsum(
        "ilf,ilr->ifr", activation, grad_fc2_rank, preferred_element_type=jnp.float32
    )
    normal_cdf = 0.5 * (1.0 + lax.erf(preact * (1.0 / math.sqrt(2.0))))
    normal_density = jnp.exp(-0.5 * preact * preact) * (1.0 / math.sqrt(2.0 * math.pi))
    grad_preact = (grad_activation * (normal_cdf + preact * normal_density)).astype(jnp.bfloat16)
    fc1_up_part = jnp.einsum(
        "ilr,ilf->irf", fc1_rank, grad_preact, preferred_element_type=jnp.float32
    )
    normed_two_part = jnp.einsum(
        "ilf,df->ild", grad_preact, fc1_back, preferred_element_type=jnp.float32
    )
    fc1_rank_part = jnp.einsum(
        "ilf,irf->ilr", grad_preact, sel_fc1, preferred_element_type=jnp.float32
    )
    grad_normed_two, grad_fc1_total = lax.psum((normed_two_part, fc1_rank_part), "tensor")
    grad_fc1_rank = grad_fc1_total.astype(jnp.bfloat16)
    grad_normed_two = grad_normed_two + jnp.einsum(
        "ilr,idr->ild", grad_fc1_rank, sel_down[:, 3], preferred_element_type=jnp.float32
    )
    fc1_down_part = jnp.einsum(
        "ild,ilr->idr", normed_two_low, grad_fc1_rank, preferred_element_type=jnp.float32
    )
    grad_hidden = upstream + norm_back(grad_normed_two, unit_two, inverse_two, ln2_gain)
    qkv_back, proj_back = (
        lax.all_gather(w_qkv, ("shard", "context"), axis=0, tiled=True),
        lax.all_gather(w_proj, ("shard", "context"), axis=0, tiled=True),
    )
    grad_attn = (grad_hidden * layer_scale[0]).astype(jnp.bfloat16)
    grad_proj_rank = jnp.einsum(
        "ild,ird->ilr", grad_attn, sel_out[:, 0], preferred_element_type=jnp.float32
    ).astype(jnp.bfloat16)
    out_grad_proj = jnp.einsum(
        "ilr,ild->ird", proj_rank, grad_attn, preferred_element_type=jnp.float32
    )
    grad_mixed = jnp.einsum("ild,dc->ilc", grad_attn, proj_back, preferred_element_type=jnp.float32)
    grad_mixed = grad_mixed + jnp.einsum(
        "ilr,icr->ilc", grad_proj_rank, sel_proj, preferred_element_type=jnp.float32
    )
    grad_mixed_low = grad_mixed.astype(jnp.bfloat16)
    proj_down_part = jnp.einsum(
        "ilc,ilr->icr", mixed_low, grad_proj_rank, preferred_element_type=jnp.float32
    )
    keys_back, values_back = (keys_all, values_all)
    key_heads_back = keys_back.reshape(images, -1, head_count, HEAD_DIM)
    value_heads_back = values_back.reshape(images, -1, head_count, HEAD_DIM)
    grad_heads = grad_mixed_low.reshape(images, row_count, head_count, HEAD_DIM)
    scores_again = (
        jnp.einsum("iqhe,ikhe->ihqk", queries, key_heads_back, preferred_element_type=jnp.float32)
        * score_scale
    )
    probs_again = jnp.exp(scores_again - log_total)
    grad_probs = jnp.einsum(
        "iqhe,ikhe->ihqk", grad_heads, value_heads_back, preferred_element_type=jnp.float32
    )
    row_inner = jnp.sum(probs_again * grad_probs, axis=-1, keepdims=True)
    grad_scores = (probs_again * (grad_probs - row_inner)).astype(jnp.bfloat16)
    grad_queries = (
        jnp.einsum(
            "ihqk,ikhe->iqhe", grad_scores, key_heads_back, preferred_element_type=jnp.float32
        )
        * score_scale
    )
    key_part = (
        jnp.einsum("ihqk,iqhe->ikhe", grad_scores, queries, preferred_element_type=jnp.float32)
        * score_scale
    )
    value_part = jnp.einsum(
        "ihqk,iqhe->ikhe",
        probs_again.astype(jnp.bfloat16),
        grad_heads,
        preferred_element_type=jnp.float32,
    )
    key_grad, value_grad = (
        lax.psum_scatter(
            key_part.reshape(images, -1, local_width), "context", scatter_dimension=1, tiled=True
        ),
        lax.psum_scatter(
            value_part.reshape(images, -1, local_width), "context", scatter_dimension=1, tiled=True
        ),
    )
    grad_projected = jnp.stack(
        [grad_queries.reshape(images, row_count, local_width), key_grad, value_grad], axis=1
    ).astype(jnp.bfloat16)
    qkv_up_part = jnp.einsum(
        "iklr,iklc->ikrc", rank_qkv, grad_projected, preferred_element_type=jnp.float32
    )
    normed_part = jnp.einsum(
        "iklc,dkc->ild", grad_projected, qkv_back, preferred_element_type=jnp.float32
    )
    rank_part = jnp.einsum(
        "iklc,ikrc->iklr", grad_projected, sel_qkv, preferred_element_type=jnp.float32
    )
    grad_normed, grad_rank_total = lax.psum((normed_part, rank_part), "tensor")
    grad_rank = grad_rank_total.astype(jnp.bfloat16)
    grad_normed = grad_normed + jnp.einsum(
        "iklr,ikdr->ild", grad_rank, sel_down[:, :3], preferred_element_type=jnp.float32
    )
    qkv_down_part = jnp.einsum(
        "ild,iklr->ikdr", normed_low, grad_rank, preferred_element_type=jnp.float32
    )
    input_grad = grad_hidden + norm_back(grad_normed, unit_one, inverse_one, ln1_gain)
    down_total = collect(jnp.concatenate([qkv_down_part, fc1_down_part[:, None]], axis=1))
    qkv_up_total = collect(qkv_up_part)
    fc1_up_total = collect(fc1_up_part)
    proj_down_total = collect(proj_down_part)
    fc2_down_total = collect(fc2_down_part)
    out_up_total = collect(jnp.stack([out_grad_proj, out_grad_fc2], axis=1))
    adapter_sums = lax.psum(
        (down_total, qkv_up_total, fc1_up_total, proj_down_total, fc2_down_total, out_up_total),
        ("shard", "context"),
    )
    return (
        result,
        input_grad,
        adapter_sums[0],
        adapter_sums[1],
        adapter_sums[2],
        adapter_sums[3],
        adapter_sums[4],
        adapter_sums[5],
    )


def solution(mesh):
    placed = (
        P("shard", "context", None),
        P("shard", "context", None),
        P("shard"),
        P(),
        P(),
        P(),
        P(),
        P(),
        P(("shard", "context"), None, "tensor"),
        P(("shard", "context"), "tensor"),
        P(("shard", "context"), "tensor"),
        P(("shard", "context"), "tensor"),
        P(),
        P(None, None, None, "tensor"),
        P(None, None, "tensor"),
        P(None, "tensor", None),
        P(None, "tensor", None),
        P(),
    )
    return jax.shard_map(
        per_device,
        mesh=mesh,
        in_specs=placed,
        out_specs=(
            P("shard", "context", None),
            P("shard", "context", None),
            P(),
            P(None, None, None, "tensor"),
            P(None, None, "tensor"),
            P(None, "tensor", None),
            P(None, "tensor", None),
            P(),
        ),
        check_vma=False,
    )
```

profile of v0, /device:TPU:0, one launch (start us, length us, event | category | flops | bytes accessed | tf_op | source)
XLA Modules:
  0.0 1194.9 jit_solution(3190369262834206231)
XLA Ops:
  17.8 40.0 %all-gather.8.cloned.1.call-done = bf16[1024,3,256]{0,2,1:T(8,128)(2,1)} async-done(((bf16[128,3,256]{0,2,1:T(8,128)(2,1)}), bf16[1024,3,256]{0,2,1:T(8,128)(2,1)}) %all-gather.8.cloned.1.call-update) | async-done | bytes 1572880 | tf_op jit(solution)/shard_map/all_gather | solution.py:69
  68.1 32.2 %all_gather.25 = bf16[1024,256]{1,0:T(8,128)(2,1)S(1)} all-gather(bf16[128,256]{1,0:T(8,128)(2,1)S(1)} %copy-done.55), channel_id=1, replica_groups=mesh['shard'=4,'context'=2,'tensor'=4] {'shard','context'}, dimensions={0}, use_global_device_ids=true | all-gather | bytes 589824 | tf_op jit(solution)/shard_map/all_gather | solution.py:70
  106.4 15.7 %multiply_reduce_fusion.1 = (f32[4,4,512]{2,1,0:T(4,128)S(1)}, f32[4,4,512,1024]{3,2,1,0:T(8,128)}) fusion(bf16[4,512,4,64]{1,3,2,0:T(8,128)(2,1)S(1)} %bitcast.147, bf16[4,1024,4,64]{1,3,2,0:T(8,128)(2,1)} %bitcast.149), kind=kOutput, calls=%fused_computation.6 | convolution fusion | flops 1090510848 | bytes 36732928 | tf_op jit(solution)/shard_map/iqhe,ikhe->ihqk/dot_general | solution.py:99
  122.2 14.2 %fusion = f32[4,4,512]{2,1,0:T(4,128)S(1)} fusion(f32[4,4,512,1024]{3,2,1,0:T(8,128)} %get-tuple-element.38, f32[4,4,512]{2,1,0:T(4,128)S(1)} %get-tuple-element.37), kind=kLoop, calls=%fused_computation.5 | loop fusion | flops 25157632 | bytes 33619968 | tf_op jit(solution)/shard_map/reduce_sum | solution.py:104
  141.1 14.4 %fusion.55 = bf16[4,4,64,512]{3,2,1,0:T(8,128)(2,1)S(1)} fusion(bf16[4,1024,4,64]{1,3,2,0:T(8,128)(2,1)} %bitcast.153, f32[4,4,512,1024]{3,2,1,0:T(8,128)} %get-tuple-element.38, f32[4,4,512]{2,1,0:T(4,128)S(1)} %fusion, f32[4,4,512]{2,1,0:T(4,128)S(1)} %get-tuple-element.37), kind=kOutput, calls=%fused_computation.92 | convolution fusion | flops 1107820544 | bytes 36765696 | tf_op jit(solution)/shard_map/ihqk,ikhe->iqhe/dot_general | solution.py:107
  167.3 24.9 %all-gather.12.cloned.1.call-done = bf16[1024,1024]{1,0:T(8,128)(2,1)} async-done(((bf16[128,1024]{1,0:T(8,128)(2,1)}), bf16[1024,1024]{1,0:T(8,128)(2,1)}) %all-gather.12.cloned.1.call-update) | async-done | bytes 2097168 | tf_op jit(solution)/shard_map/all_gather | solution.py:74
  192.2 10.7 fusion.42
  203.1 15.5 %all-reduce.20 = bf16[4,512,16]{1,2,0:T(8,128)(2,1)S(1)} all-reduce(f32[4,512,16]{1,2,0:T(8,128)S(1)} %fusion.110), channel_id=1, replica_groups=mesh['shard'=4,'context'=2,'tensor'=4] {'tensor'}, use_global_device_ids=true, to_apply=%region_5.0 | all-reduce | flops 32768 | bytes 196608 | tf_op jit(solution)/shard_map/psum | solution.py:115
  218.6 130.0 %all-reduce.11.cloned.1.call-done = f32[4,512,1024]{2,1,0:T(8,128)} async-done(((f32[4,512,1024]{2,1,0:T(8,128)}), f32[4,512,1024]{2,1,0:T(8,128)}) %all-reduce.11.cloned.1.call-update) | async-done | bytes 8388624 | tf_op jit(solution)/shard_map/psum | solution.py:115
  348.6 6.4 fusion.137
  361.6 38.2 %all-gather.10.cloned.1.call-done = bf16[1024,1024]{1,0:T(8,128)(2,1)} async-done(((bf16[128,1024]{1,0:T(8,128)(2,1)}), bf16[1024,1024]{1,0:T(8,128)(2,1)}) %all-gather.10.cloned.1.call-update) | async-done | bytes 2097168 | tf_op jit(solution)/shard_map/all_gather | solution.py:73
  399.9 6.9 fusion.48
  412.3 9.0 fusion.28
  423.4 6.9 fusion.46
  434.1 15.3 %all-reduce.21 = bf16[4,512,16]{1,2,0:T(8,128)(2,1)S(1)} all-reduce(f32[4,512,16]{1,2,0:T(8,128)S(1)} %fusion.89), channel_id=1, replica_groups=mesh['shard'=4,'context'=2,'tensor'=4] {'tensor'}, use_global_device_ids=true, to_apply=%region_11.0 | all-reduce | flops 32768 | bytes 196608 | tf_op jit(solution)/shard_map/psum | solution.py:177
  449.4 134.7 %all-reduce.13.cloned.1.call-done = f32[4,512,1024]{2,1,0:T(8,128)} async-done(((f32[4,512,1024]{2,1,0:T(8,128)}), f32[4,512,1024]{2,1,0:T(8,128)}) %all-reduce.13.cloned.1.call-update) | async-done | bytes 8388624 | tf_op jit(solution)/shard_map/psum | solution.py:177
  584.1 7.4 fusion.134
  591.6 8.1 multiply_convert_fusion.1
  603.5 15.4 %fusion.2 = f32[4,4,64,1024]{3,2,1,0:T(8,128)} fusion(bf16[4,512,4,64]{1,3,2,0:T(8,128)(2,1)S(1)} %bitcast.145, f32[4,4,512,1024]{3,2,1,0:T(8,128)} %get-tuple-element.38, f32[4,4,512]{2,1,0:T(4,128)S(1)} %bitcast.155), kind=kOutput, calls=%fused_computation.8 | convolution fusion | flops 1098907648 | bytes 38830080 | tf_op jit(solution)/shard_map/ihqk,iqhe->ikhe/dot_general | solution.py:229
  624.8 22.9 %multiply_reduce_fusion = (f32[4,4,512]{2,1,0:T(4,128)S(1)}, f32[4,4,512,1024]{3,2,1,0:T(8,128)}) fusion(f32[4,4,512,1024]{3,2,1,0:T(8,128)} %get-tuple-element.38, f32[4,4,512]{2,1,0:T(4,128)S(1)} %bitcast.156, bf16[4,512,4,64]{1,3,2,0:T(8,128)(2,1)S(1)} %bitcast.146, bf16[4,1024,4,64]{1,3,2,0:T(8,128)(2,1)S(1)} %bitcast.154), kind=kOutput, calls=%fused_computation.1 | convolution fusion | flops 1107288064 | bytes 70320128 | tf_op jit(solution)/shard_map/iqhe,ikhe->ihqk/dot_general | solution.py:214
  647.7 28.5 %multiply_convert_fusion = bf16[4,4,512,1024]{3,2,1,0:T(8,128)(2,1)} fusion(f32[4,4,512,1024]{3,2,1,0:T(8,128)} %get-tuple-element.44, f32[4,4,512,1024]{3,2,1,0:T(8,128)} %get-tuple-element.38, f32[4,4,512]{2,1,0:T(4,128)S(1)} %get-tuple-element.43, f32[4,4,512]{2,1,0:T(4,128)S(1)} %bitcast.157), kind=kLoop, calls=%fused_computation | loop fusion | flops 41943040 | bytes 83951616 | tf_op jit(solution)/shard_map/convert_element_type | solution.py:218
  676.2 10.9 broadcast_multiply_fusion
  696.6 20.4 %fusion.22 = bf16[4,512,1024]{2,1,0:T(8,128)(2,1)S(1)} fusion(f32[4,512,1024]{2,1,0:T(8,128)} %copy-done.17, u8[512,1024]{1,0:T(8,128)(4,1)S(1)} %copy-done.31, u8[512,1024]{1,0:T(8,128)(4,1)S(1)} %copy-done.30), kind=kLoop, calls=%fused_computation.34 | loop fusion | flops 146800640 | bytes 13631488 | tf_op jit(solution)/shard_map/convert_element_type | solution.py:130
  726.7 11.0 multiply_convert_fusion.2
  740.8 6.4 reduce-scatter.3.cloned.1.call-done
  748.9 8.8 convolution_bitcast_fusion
  764.3 72.5 %all-reduce.19.cloned.1.call-done = (bf16[4,512,1024]{2,1,0:T(8,128)(2,1)}, bf16[4,512,16]{1,2,0:T(8,128)(2,1)}) async-done(((bf16[4,512,1024]{2,1,0:T(8,128)(2,1)}, bf16[4,512,16]{1,2,0:T(8,128)(2,1)}), (bf16[4,512,1024]{2,1,0:T(8,128)(2,1)}, bf16[4,512,16]{1,2,0:T(8,128)(2,1)})) %all-reduce.19.cloned.1.call-update) | async-done | bytes 4259856 | tf_op jit(solution)/shard_map/psum | solution.py:136
  848.5 22.0 %all-reduce.22 = bf16[4,3,512,16]{2,3,1,0:T(8,128)(2,1)S(1)} all-reduce(f32[4,3,512,16]{2,3,1,0:T(8,128)S(1)} %fusion.99), channel_id=1, replica_groups=mesh['shard'=4,'context'=2,'tensor'=4] {'tensor'}, use_global_device_ids=true, to_apply=%region_18.0 | all-reduce | flops 98304 | bytes 589824 | tf_op jit(solution)/shard_map/psum | solution.py:255
  879.9 8.5 add_convert_fusion
  888.4 110.2 %all-reduce.15.cloned.1.call-done = f32[4,512,1024]{2,1,0:T(8,128)} async-done(((f32[4,512,1024]{2,1,0:T(8,128)}), f32[4,512,1024]{2,1,0:T(8,128)}) %all-reduce.15.cloned.1.call-update) | async-done | bytes 8388624 | tf_op jit(solution)/shard_map/psum | solution.py:255
  1005.7 12.8 %fusion.17 = f32[4,512,1024]{2,1,0:T(8,128)} fusion(bf16[4,512,1024]{2,1,0:T(8,128)(2,1)S(1)} %copy-done.4, f32[4,512,1024]{2,1,0:T(8,128)S(1)} %get-tuple-element.45, f32[4,512]{1,0:T(4,128)S(1)} %broadcast_multiply_fusion.1, f32[4,512]{1,0:T(4,128)S(1)} %broadcast_multiply_fusion.2, f32[4,512]{1,0:T(4,128)S(1)} %copy-done.37, f32[4,512]{1,0:T(4,128)S(1)} %copy-done.33, ...), kind=kLoop, calls=%fused_computation.29 | loop fusion | flops 33554432 | bytes 42008576 | tf_op jit(solution)/shard_map/add | solution.py:263
  1018.5 154.7 %all-reduce.17.cloned.1.call-done = (f32[8,4,1024,16]{2,0,3,1:T(8,128)}, f32[8,3,16,256]{3,0,2,1:T(8,128)}, f32[8,16,1024]{2,0,1:T(8,128)}, f32[8,256,16]{1,0,2:...) async-done(((f32[8,4,1024,16]{2,0,3,1:T(8,128)}, f32[8,3,16,256]{3,0,2,1:T(8,128)}, f32[8,16,1024]{2,0,1:T(8,128)}, f32[8,256,16]{1,0,2:T(8,128)}, ...) | async-done | bytes 4718608 | tf_op jit(solution)/shard_map/psum | solution.py:270
  (235 shorter events, 143.9 us)
Async XLA Ops:
  7.2 50.6 %all-gather.8.cloned.1.call-start = ((), (), s32[]{:S(2)}) async-start(), calls=%async_computation.2 | async-start | bytes 1769472 | tf_op jit(solution)/shard_map/all_gather | solution.py:69
  9.1 97.3 %all-gather.16.cloned.1.call-start = ((), (), s32[]{:S(2)}) async-start(), calls=%async_computation.11 | async-start | bytes 3145728 | tf_op jit(solution)/shard_map/all_gather | solution.py:93
  13.9 43.9 %copy-start.32 = (f32[4,512]{1,0:T(4,128)}, f32[4,512]{1,0:T(4,128)S(1)}, u32[]{:S(2)}) copy-start(f32[4,512]{1,0:T(4,128)S(1)} %broadcast_multiply_fusion.6) | copy-start | bytes 24580
  15.4 42.5 %copy-start.36 = (f32[4,512]{1,0:T(4,128)}, f32[4,512]{1,0:T(4,128)S(1)}, u32[]{:S(2)}) copy-start(f32[4,512]{1,0:T(4,128)S(1)} %add_rsqrt_fusion.1) | copy-start | bytes 24580
  15.7 48.3 %copy-start.34 = (bf16[4,3,16,256]{3,0,2,1:T(4,128)(2,1)}, bf16[4,3,16,256]{3,0,2,1:T(4,128)(2,1)S(1)}, u32[]{:S(2)}) copy-start(bf16[4,3,16,256]{3,0,2,1:T(4,128)(2,1)S(1)} %convolution_convert_fusion.6) | copy-start | bytes 294916
  17.8 46.1 %copy-start.45 = (bf16[4,3,16,512]{3,2,1,0:T(8,128)(2,1)}, bf16[4,3,16,512]{3,2,1,0:T(8,128)(2,1)S(1)}, u32[]{:S(2)}) copy-start(bf16[4,3,16,512]{3,2,1,0:T(8,128)(2,1)S(1)} %convolution_convert_fusion.3) | copy-start | bytes 589828
  66.7 55.5 %copy-start.15 = (bf16[4,1,512,256]{2,3,1,0:T(8,128)(2,1)}, bf16[4,1,512,256]{2,3,1,0:T(8,128)(2,1)S(1)}, u32[]{:S(2)}) copy-start(bf16[4,1,512,256]{2,3,1,0:T(8,128)(2,1)S(1)} %get-tuple-element.31) | copy-start | bytes 3145732
  66.7 74.4 %all-gather.14.cloned.1.call-start = ((), (), s32[]{:S(2)}) async-start(), calls=%async_computation.10 | async-start | bytes 3145728 | tf_op jit(solution)/shard_map/all_gather | solution.py:94
  67.5 124.8 %all-gather.12.cloned.1.call-start = ((), (), s32[]{:S(2)}) async-start(), calls=%async_computation.5 | async-start | bytes 2359296 | tf_op jit(solution)/shard_map/all_gather | solution.py:74
  68.0 280.6 %all-reduce.11.cloned.1.call-start = ((), (), s32[]{:S(2)}) async-start(), calls=%async_computation.3 | async-start | bytes 16777216 | tf_op jit(solution)/shard_map/psum | solution.py:115
  155.5 47.4 %copy-start.13 = (bf16[4,4,64,512]{3,2,1,0:T(8,128)(2,1)}, bf16[4,4,64,512]{3,2,1,0:T(8,128)(2,1)S(1)}, u32[]{:S(2)}) copy-start(bf16[4,4,64,512]{3,2,1,0:T(8,128)(2,1)S(1)} %fusion.55) | copy-start | bytes 3145732
  160.3 239.6 %all-gather.10.cloned.1.call-start = ((), (), s32[]{:S(2)}) async-start(), calls=%async_computation.4 | async-start | bytes 2359296 | tf_op jit(solution)/shard_map/all_gather | solution.py:73
  160.9 423.2 %all-reduce.13.cloned.1.call-start = ((), (), s32[]{:S(2)}) async-start(), calls=%async_computation.6 | async-start | bytes 16777216 | tf_op jit(solution)/shard_map/psum | solution.py:177
  167.3 245.0 %copy-start.47 = (bf16[4,512,16]{1,2,0:T(8,128)(2,1)}, bf16[4,512,16]{1,2,0:T(8,128)(2,1)S(1)}, u32[]{:S(2)}) copy-start(bf16[4,512,16]{1,2,0:T(8,128)(2,1)S(1)} %fusion.59) | copy-start | bytes 196612
  218.6 136.4 %copy-start.25 = (bf16[4,512,16]{1,2,0:T(8,128)(2,1)}, bf16[4,512,16]{1,2,0:T(8,128)(2,1)S(1)}, u32[]{:S(2)}) copy-start(bf16[4,512,16]{1,2,0:T(8,128)(2,1)S(1)} %all-reduce.20) | copy-start | bytes 196612
  355.1 236.5 %copy-start.38 = (f32[4,512]{1,0:T(4,128)}, f32[4,512]{1,0:T(4,128)S(1)}, u32[]{:S(2)}) copy-start(f32[4,512]{1,0:T(4,128)S(1)} %broadcast_multiply_fusion.5) | copy-start | bytes 24580
  356.3 235.3 %copy-start.42 = (f32[4,512]{1,0:T(4,128)}, f32[4,512]{1,0:T(4,128)S(1)}, u32[]{:S(2)}) copy-start(f32[4,512]{1,0:T(4,128)S(1)} %add_rsqrt_fusion) | copy-start | bytes 24580
  430.4 308.7 %reduce-scatter.5.cloned.1.call-start = ((), (), s32[]{:S(2)}) async-start(), calls=%async_computation.8 | async-start | bytes 6291456 | tf_op jit(solution)/shard_map/reduce_scatter | solution.py:239
  624.5 122.8 %reduce-scatter.3.cloned.1.call-start = ((), (), s32[]{:S(2)}) async-start(), calls=%async_computation.7 | async-start | bytes 6291456 | tf_op jit(solution)/shard_map/reduce_scatter | solution.py:236
  692.6 144.2 %all-reduce.19.cloned.1.call-start = ((), (), s32[]{:S(2)}) async-start(), calls=%async_computation.13 | async-start | bytes 8519680 | tf_op jit(solution)/shard_map/psum | solution.py:136
  726.5 272.1 %all-reduce.15.cloned.1.call-start = ((), (), s32[]{:S(2)}) async-start(), calls=%async_computation.9 | async-start | bytes 16777216 | tf_op jit(solution)/shard_map/psum | solution.py:255
  757.7 79.1 %copy-start.61 = (f32[1,1024]{1,0:T(1,128)S(1)}, f32[1,1024]{1,0:T(1,128)}, u32[]{:S(2)}) copy-start(f32[1,1024]{1,0:T(1,128)} %copy-done.60) | copy-start | bytes 12292
  757.7 82.2 %copy-start.26 = (bf16[4,512,16]{1,2,0:T(8,128)(2,1)S(1)}, bf16[4,512,16]{1,2,0:T(8,128)(2,1)}, u32[]{:S(2)}) copy-start(bf16[4,512,16]{1,2,0:T(8,128)(2,1)} %copy-done.25) | copy-start | bytes 196612
  757.7 415.5 %all-reduce.17.cloned.1.call-start = ((), (), s32[]{:S(2)}) async-start(), calls=%async_computation.12 | async-start | bytes 9437184 | tf_op jit(solution)/shard_map/psum | solution.py:270
  759.9 82.9 %copy-start.14 = (bf16[4,4,64,512]{3,2,1,0:T(8,128)(2,1)S(1)}, bf16[4,4,64,512]{3,2,1,0:T(8,128)(2,1)}, u32[]{:S(2)}) copy-start(bf16[4,4,64,512]{3,2,1,0:T(8,128)(2,1)} %copy-done.13) | copy-start | bytes 3145732
  879.9 118.7 %copy-start.21 = (bf16[4,3,1024,16]{2,0,3,1:T(4,128)(2,1)S(1)}, bf16[4,3,1024,16]{2,0,3,1:T(4,128)(2,1)}, u32[]{:S(2)}) copy-start(bf16[4,3,1024,16]{2,0,3,1:T(4,128)(2,1)} %copy-done.20) | copy-start | bytes 1179652
  879.9 118.7 %copy-start.59 = (f32[1024]{0:T(1024)S(1)}, f32[1024]{0:T(1024)}, u32[]{:S(2)}) copy-start(f32[1024]{0:T(1024)} %param.21) | copy-start | bytes 12292
  888.4 116.6 %copy-start.39 = (f32[4,512]{1,0:T(4,128)S(1)}, f32[4,512]{1,0:T(4,128)}, u32[]{:S(2)}) copy-start(f32[4,512]{1,0:T(4,128)} %copy-done.38) | copy-start | bytes 24580
  888.4 116.6 %copy-start.43 = (f32[4,512]{1,0:T(4,128)S(1)}, f32[4,512]{1,0:T(4,128)}, u32[]{:S(2)}) copy-start(f32[4,512]{1,0:T(4,128)} %copy-done.42) | copy-start | bytes 24580
  888.4 116.6 %copy-start.49 = (f32[4,512]{1,0:T(4,128)S(1)}, f32[4,512]{1,0:T(4,128)}, u32[]{:S(2)}) copy-start(f32[4,512]{1,0:T(4,128)} %copy-done.48) | copy-start | bytes 24580
  888.4 116.6 %copy-start.51 = (f32[4,512]{1,0:T(4,128)S(1)}, f32[4,512]{1,0:T(4,128)}, u32[]{:S(2)}) copy-start(f32[4,512]{1,0:T(4,128)} %copy-done.50) | copy-start | bytes 24580
  1005.7 182.2 %copy-start.1 = (bf16[8,4,1024,16]{2,3,1,0:T(8,128)(2,1)S(1)}, bf16[8,4,1024,16]{2,3,1,0:T(8,128)(2,1)}, u32[]{:S(2)}) copy-start(bf16[8,4,1024,16]{2,3,1,0:T(8,128)(2,1)} %param.30) | copy-start | bytes 3145732
  (50 other events, 480.3 us)
Sparse Core Ops, SparseCore 0:
  10.7 47.1 all-gather.7
  66.8 39.5 all-gather.15
  108.6 32.5 all-gather.13
  143.1 49.0 all-gather.11
  195.1 153.4 all-reduce.10
  350.6 49.2 all-gather.9
  430.5 153.5 all-reduce.12
  624.6 54.5 reduce-scatter.4
  692.7 54.4 reduce-scatter.2
  750.1 86.5 all-reduce.18
  839.2 159.3 all-reduce.14
  1003.2 169.8 all-reduce.16
where the time goes:
time: 1200 us; the launch traced here: 1190 us
  waiting for transfers between devices  724 us (60%)
  matrix products  234 us (20%)
  other arithmetic  94.5 us (8%)
  blocking collectives  85.1 us (7%)
  local copies, waits for them, and re-layouts  39.2 us (3%)
  between operations  15.4 us (1%)
    psum x1, waiting for transfers between devices, per_device(): lax.psum((down_total, qkv_up_total, fc1_up_total, proj_down_total, fc2_do...  155 us
    psum x1, waiting for transfers between devices, per_device(): lax.psum((normed_two_part, fc1_rank_part), 'tensor')  135 us
    psum x1, waiting for transfers between devices, per_device(): lax.psum((proj_part, proj_rank_part), 'tensor')  130 us
    psum x1, waiting for transfers between devices, per_device(): grad_normed, grad_rank_total = lax.psum((normed_part, rank_part), 'tensor')  110 us
    psum x1, waiting for transfers between devices, per_device(): lax.psum(mlp_part.astype(jnp.bfloat16), 'tensor').astype(jnp.float32)  72.5 us
    all_gather x1, waiting for transfers between devices, per_device(): lax.all_gather(w_qkv, ('shard', 'context'), axis=0, tiled=True)  40 us
    all_gather x1, waiting for transfers between devices, per_device(): lax.all_gather(w_fc1, ('shard', 'context'), axis=0, tiled=True)  38.2 us
    all_gather x1, blocking collectives, per_device(): lax.all_gather(w_proj, ('shard', 'context'), axis=0, tiled=True)  32.2 us
  transfers between devices with their start and end apart: 12, of which 11 were waited for; matrix products, arithmetic and copies ran while one was open for 22% of the time, Pallas kernels for 0%

commit v1 on v0

--- a/solution.py
+++ b/solution.py
@@ -133,7 +133,9 @@
         "ilf,ifr->ilr", activation, sel_fc2, preferred_element_type=jnp.float32
     )
     mlp_total, fc2_rank_total = (
-        lax.psum(mlp_part.astype(jnp.bfloat16), "tensor").astype(jnp.float32),
+        jnp.sum(
+            jax.lax.all_gather(mlp_part.astype(jnp.bfloat16), axis_name="tensor"), axis=0
+        ).astype(jnp.float32),
         lax.psum(fc2_rank_part.astype(jnp.bfloat16), "tensor").astype(jnp.float32),
     )
     fc2_rank = fc2_rank_total.astype(jnp.bfloat16)

time: 1200 us -> 1260 us (1.050)
  waiting for transfers between devices: 724 us -> 766 us
    all_gather x0 -> x1, waiting for transfers between devices: none -> 91.3 us  [per_device(): jax.lax.all_gather(mlp_part.astype(jnp.bfloat16), axis_name='tensor')]
    psum x1, waiting for transfers between devices: 72.5 us -> 16.7 us  [per_device(): lax.psum(fc2_rank_part.astype(jnp.bfloat16), 'tensor').astype(jnp.float32)]
    unnamed x147 -> x139, local copies, waits for them, and re-layouts: 24.2 us -> 26.1 us
  transfers between devices with their start and end apart: 12 -> 13, of which waited for: 11 -> 12; matrix products, arithmetic and copies ran while one was open for 22% -> 22% of each run, Pallas kernels for 0% -> 0%
where the time goes in v1:
time: 1260 us; the launch traced here: 1250 us
  waiting for transfers between devices  766 us (61%)
  matrix products  238 us (19%)
  other arithmetic  106 us (8%)
  blocking collectives  84.6 us (7%)
  local copies, waits for them, and re-layouts  41 us (3%)
  between operations  15 us (1%)
    psum x1, waiting for transfers between devices, per_device(): lax.psum((down_total, qkv_up_total, fc1_up_total, proj_down_total, fc2_do...  155 us
    psum x1, waiting for transfers between devices, per_device(): lax.psum((normed_two_part, fc1_rank_part), 'tensor')  134 us
    psum x1, waiting for transfers between devices, per_device(): lax.psum((proj_part, proj_rank_part), 'tensor')  130 us
    psum x1, waiting for transfers between devices, per_device(): grad_normed, grad_rank_total = lax.psum((normed_part, rank_part), 'tensor')  113 us
    all_gather x1, waiting for transfers between devices, per_device(): jax.lax.all_gather(mlp_part.astype(jnp.bfloat16), axis_name='tensor')  91.3 us
    all_gather x1, waiting for transfers between devices, per_device(): lax.all_gather(w_qkv, ('shard', 'context'), axis=0, tiled=True)  40 us
    all_gather x1, waiting for transfers between devices, per_device(): lax.all_gather(w_fc1, ('shard', 'context'), axis=0, tiled=True)  38.3 us
    all_gather x1, blocking collectives, per_device(): lax.all_gather(w_proj, ('shard', 'context'), axis=0, tiled=True)  32.4 us
  transfers between devices with their start and end apart: 13, of which 12 were waited for; matrix products, arithmetic and copies ran while one was open for 22% of the time, Pallas kernels for 0%

profile of v1, /device:TPU:0, one launch (start us, length us, event | category | flops | bytes accessed | tf_op | source)
XLA Modules:
  0.0 1251.9 jit_solution(9301459188650260766)
XLA Ops:
  17.8 40.0 %all-gather.10.cloned.1.call-done = bf16[1024,3,256]{0,2,1:T(8,128)(2,1)} async-done(((bf16[128,3,256]{0,2,1:T(8,128)(2,1)}), bf16[1024,3,256]{0,2,1:T(8,128)(2,1)}) %all-gather.10.cloned.1.call-update) | async-done | bytes 1572880 | tf_op jit(solution)/shard_map/all_gather | solution.py:69
  68.1 32.4 %all_gather.31 = bf16[1024,256]{1,0:T(8,128)(2,1)S(1)} all-gather(bf16[128,256]{1,0:T(8,128)(2,1)S(1)} %copy-done.51), channel_id=1, replica_groups=mesh['shard'=4,'context'=2,'tensor'=4] {'shard','context'}, dimensions={0}, use_global_device_ids=true | all-gather | bytes 589824 | tf_op jit(solution)/shard_map/all_gather | solution.py:70
  106.6 15.7 %multiply_reduce_fusion.1 = (f32[4,4,512]{2,1,0:T(4,128)S(1)}, f32[4,4,512,1024]{3,2,1,0:T(8,128)}) fusion(bf16[4,512,4,64]{1,3,2,0:T(8,128)(2,1)S(1)} %bitcast.149, bf16[4,1024,4,64]{1,3,2,0:T(8,128)(2,1)} %bitcast.151), kind=kOutput, calls=%fused_computation.6 | convolution fusion | flops 1090510848 | bytes 36732928 | tf_op jit(solution)/shard_map/iqhe,ikhe->ihqk/dot_general | solution.py:99
  122.3 14.2 %fusion = f32[4,4,512]{2,1,0:T(4,128)S(1)} fusion(f32[4,4,512,1024]{3,2,1,0:T(8,128)} %get-tuple-element.44, f32[4,4,512]{2,1,0:T(4,128)S(1)} %get-tuple-element.43), kind=kLoop, calls=%fused_computation.5 | loop fusion | flops 25157632 | bytes 33619968 | tf_op jit(solution)/shard_map/reduce_sum | solution.py:104
  141.3 14.4 %fusion.55 = bf16[4,4,64,512]{3,2,1,0:T(8,128)(2,1)S(1)} fusion(bf16[4,1024,4,64]{1,3,2,0:T(8,128)(2,1)} %bitcast.155, f32[4,4,512,1024]{3,2,1,0:T(8,128)} %get-tuple-element.44, f32[4,4,512]{2,1,0:T(4,128)S(1)} %fusion, f32[4,4,512]{2,1,0:T(4,128)S(1)} %get-tuple-element.43), kind=kOutput, calls=%fused_computation.92 | convolution fusion | flops 1107820544 | bytes 36765696 | tf_op jit(solution)/shard_map/ihqk,ikhe->iqhe/dot_general | solution.py:107
  167.2 25.2 %all-gather.14.cloned.1.call-done = bf16[1024,1024]{1,0:T(8,128)(2,1)} async-done(((bf16[128,1024]{1,0:T(8,128)(2,1)}), bf16[1024,1024]{1,0:T(8,128)(2,1)}) %all-gather.14.cloned.1.call-update) | async-done | bytes 2097168 | tf_op jit(solution)/shard_map/all_gather | solution.py:74
  192.4 10.6 fusion.42
  203.3 15.5 %all-reduce.19 = bf16[4,512,16]{1,2,0:T(8,128)(2,1)S(1)} all-reduce(f32[4,512,16]{1,2,0:T(8,128)S(1)} %fusion.110), channel_id=1, replica_groups=mesh['shard'=4,'context'=2,'tensor'=4] {'tensor'}, use_global_device_ids=true, to_apply=%region_5.0 | all-reduce | flops 32768 | bytes 196608 | tf_op jit(solution)/shard_map/psum | solution.py:115
  218.9 130.0 %all-reduce.10.cloned.1.call-done = f32[4,512,1024]{2,1,0:T(8,128)} async-done(((f32[4,512,1024]{2,1,0:T(8,128)}), f32[4,512,1024]{2,1,0:T(8,128)}) %all-reduce.10.cloned.1.call-update) | async-done | bytes 8388624 | tf_op jit(solution)/shard_map/psum | solution.py:115
  361.8 38.3 %all-gather.12.cloned.1.call-done = bf16[1024,1024]{1,0:T(8,128)(2,1)} async-done(((bf16[128,1024]{1,0:T(8,128)(2,1)}), bf16[1024,1024]{1,0:T(8,128)(2,1)}) %all-gather.12.cloned.1.call-update) | async-done | bytes 2097168 | tf_op jit(solution)/shard_map/all_gather | solution.py:73
  412.6 9.0 fusion.28
  434.5 15.3 %all-reduce.20 = bf16[4,512,16]{1,2,0:T(8,128)(2,1)S(1)} all-reduce(f32[4,512,16]{1,2,0:T(8,128)S(1)} %fusion.89), channel_id=1, replica_groups=mesh['shard'=4,'context'=2,'tensor'=4] {'tensor'}, use_global_device_ids=true, to_apply=%region_11.0 | all-reduce | flops 32768 | bytes 196608 | tf_op jit(solution)/shard_map/psum | solution.py:179
  449.9 134.4 %all-reduce.14.cloned.1.call-done = f32[4,512,1024]{2,1,0:T(8,128)} async-done(((f32[4,512,1024]{2,1,0:T(8,128)}), f32[4,512,1024]{2,1,0:T(8,128)}) %all-reduce.14.cloned.1.call-update) | async-done | bytes 8388624 | tf_op jit(solution)/shard_map/psum | solution.py:179
  584.3 7.4 fusion.134
  592.5 7.4 multiply_convert_fusion.1
  603.7 15.3 %fusion.2 = f32[4,4,64,1024]{3,2,1,0:T(8,128)} fusion(bf16[4,512,4,64]{1,3,2,0:T(8,128)(2,1)S(1)} %bitcast.147, f32[4,4,512,1024]{3,2,1,0:T(8,128)} %get-tuple-element.44, f32[4,4,512]{2,1,0:T(4,128)S(1)} %bitcast.157), kind=kOutput, calls=%fused_computation.8 | convolution fusion | flops 1098907648 | bytes 38830080 | tf_op jit(solution)/shard_map/ihqk,iqhe->ikhe/dot_general | solution.py:231
  624.8 22.9 %multiply_reduce_fusion = (f32[4,4,512]{2,1,0:T(4,128)S(1)}, f32[4,4,512,1024]{3,2,1,0:T(8,128)}) fusion(f32[4,4,512,1024]{3,2,1,0:T(8,128)} %get-tuple-element.44, f32[4,4,512]{2,1,0:T(4,128)S(1)} %bitcast.158, bf16[4,512,4,64]{1,3,2,0:T(8,128)(2,1)S(1)} %bitcast.148, bf16[4,1024,4,64]{1,3,2,0:T(8,128)(2,1)S(1)} %bitcast.156), kind=kOutput, calls=%fused_computation.1 | convolution fusion | flops 1107288064 | bytes 70320128 | tf_op jit(solution)/shard_map/iqhe,ikhe->ihqk/dot_general | solution.py:216
  647.7 28.5 %multiply_convert_fusion = bf16[4,4,512,1024]{3,2,1,0:T(8,128)(2,1)} fusion(f32[4,4,512,1024]{3,2,1,0:T(8,128)} %get-tuple-element.50, f32[4,4,512,1024]{3,2,1,0:T(8,128)} %get-tuple-element.44, f32[4,4,512]{2,1,0:T(4,128)S(1)} %get-tuple-element.49, f32[4,4,512]{2,1,0:T(4,128)S(1)} %bitcast.159), kind=kLoop, calls=%fused_computation | loop fusion | flops 41943040 | bytes 83951616 | tf_op jit(solution)/shard_map/convert_element_type | solution.py:220
  676.2 10.9 broadcast_multiply_fusion
  696.2 20.2 %fusion.22 = bf16[4,512,1024]{2,1,0:T(8,128)(2,1)S(1)} fusion(f32[4,512,1024]{2,1,0:T(8,128)} %copy-done.16, u8[512,1024]{1,0:T(8,128)(4,1)S(1)} %copy-done.30, u8[512,1024]{1,0:T(8,128)(4,1)S(1)} %copy-done.29), kind=kLoop, calls=%fused_computation.34 | loop fusion | flops 146800640 | bytes 13631488 | tf_op jit(solution)/shard_map/convert_element_type | solution.py:130
  723.4 11.2 multiply_convert_fusion.2
  737.7 9.5 reduce-scatter.3.cloned.1.call-done
  748.9 8.6 convolution_bitcast_fusion
  764.8 16.7 %all-reduce.12.cloned.1.call-done = bf16[4,512,16]{1,2,0:T(8,128)(2,1)} async-done(((bf16[4,512,16]{1,2,0:T(8,128)(2,1)}), bf16[4,512,16]{1,2,0:T(8,128)(2,1)}) %all-reduce.12.cloned.1.call-update) | async-done | bytes 65552 | tf_op jit(solution)/shard_map/psum | solution.py:139
  792.0 21.3 %all-reduce.21 = bf16[4,3,512,16]{2,3,1,0:T(8,128)(2,1)S(1)} all-reduce(f32[4,3,512,16]{2,3,1,0:T(8,128)S(1)} %fusion.99), channel_id=1, replica_groups=mesh['shard'=4,'context'=2,'tensor'=4] {'tensor'}, use_global_device_ids=true, to_apply=%region_18.0 | all-reduce | flops 98304 | bytes 589824 | tf_op jit(solution)/shard_map/psum | solution.py:257
  822.8 8.4 convolution_convert_fusion
  831.2 112.7 %all-reduce.16.cloned.1.call-done = f32[4,512,1024]{2,1,0:T(8,128)} async-done(((f32[4,512,1024]{2,1,0:T(8,128)}), f32[4,512,1024]{2,1,0:T(8,128)}) %all-reduce.16.cloned.1.call-update) | async-done | bytes 8388624 | tf_op jit(solution)/shard_map/psum | solution.py:257
  951.0 12.7 %fusion.17 = f32[4,512,1024]{2,1,0:T(8,128)} fusion(bf16[4,512,1024]{2,1,0:T(8,128)(2,1)S(1)} %copy-done.4, f32[4,512,1024]{2,1,0:T(8,128)S(1)} %get-tuple-element.51, f32[4,512]{1,0:T(4,128)S(1)} %broadcast_multiply_fusion.1, f32[4,512]{1,0:T(4,128)S(1)} %broadcast_multiply_fusion.2, f32[4,512]{1,0:T(4,128)S(1)} %copy-done.36, f32[4,512]{1,0:T(4,128)S(1)} %copy-done.32, ...), kind=kLoop, calls=%fused_computation.29 | loop fusion | flops 33554432 | bytes 42008576 | tf_op jit(solution)/shard_map/add | solution.py:265
  963.7 154.7 %all-reduce.18.cloned.1.call-done = (f32[8,4,1024,16]{2,0,3,1:T(8,128)}, f32[8,3,16,256]{3,0,2,1:T(8,128)}, f32[8,16,1024]{2,0,1:T(8,128)}, f32[8,256,16]{1,0,2:...) async-done(((f32[8,4,1024,16]{2,0,3,1:T(8,128)}, f32[8,3,16,256]{3,0,2,1:T(8,128)}, f32[8,16,1024]{2,0,1:T(8,128)}, f32[8,256,16]{1,0,2:T(8,128)}, ...) | async-done | bytes 4718608 | tf_op jit(solution)/shard_map/psum | solution.py:272
  1133.5 91.3 %all-gather.20.cloned.1.call-done = bf16[16,512,1024]{2,1,0:T(8,128)(2,1)} async-done(((bf16[4,512,1024]{2,1,0:T(8,128)(2,1)}), bf16[16,512,1024]{2,1,0:T(8,128)(2,1)}) %all-gather.20.cloned.1.call-update) | async-done | bytes 16777232 | tf_op jit(solution)/shard_map/all_gather | solution.py:137
  1224.8 12.1 reduce_sum.107
  1237.0 8.2 add_convert_fusion
  (231 shorter events, 161.3 us)
Async XLA Ops:
  7.2 50.6 %all-gather.10.cloned.1.call-start = ((), (), s32[]{:S(2)}) async-start(), calls=%async_computation.2 | async-start | bytes 1769472 | tf_op jit(solution)/shard_map/all_gather | solution.py:69
  9.1 97.5 %all-gather.18.cloned.1.call-start = ((), (), s32[]{:S(2)}) async-start(), calls=%async_computation.12 | async-start | bytes 3145728 | tf_op jit(solution)/shard_map/all_gather | solution.py:93
  13.9 43.9 %copy-start.31 = (f32[4,512]{1,0:T(4,128)}, f32[4,512]{1,0:T(4,128)S(1)}, u32[]{:S(2)}) copy-start(f32[4,512]{1,0:T(4,128)S(1)} %broadcast_multiply_fusion.6) | copy-start | bytes 24580
  15.4 42.5 %copy-start.35 = (f32[4,512]{1,0:T(4,128)}, f32[4,512]{1,0:T(4,128)S(1)}, u32[]{:S(2)}) copy-start(f32[4,512]{1,0:T(4,128)S(1)} %add_rsqrt_fusion.1) | copy-start | bytes 24580
  15.7 48.3 %copy-start.33 = (bf16[4,3,16,256]{3,0,2,1:T(4,128)(2,1)}, bf16[4,3,16,256]{3,0,2,1:T(4,128)(2,1)S(1)}, u32[]{:S(2)}) copy-start(bf16[4,3,16,256]{3,0,2,1:T(4,128)(2,1)S(1)} %convolution_convert_fusion.6) | copy-start | bytes 294916
  17.8 46.1 %copy-start.40 = (bf16[4,3,16,512]{3,2,1,0:T(8,128)(2,1)}, bf16[4,3,16,512]{3,2,1,0:T(8,128)(2,1)S(1)}, u32[]{:S(2)}) copy-start(bf16[4,3,16,512]{3,2,1,0:T(8,128)(2,1)S(1)} %convolution_convert_fusion.3) | copy-start | bytes 589828
  66.7 55.6 %copy-start.14 = (bf16[4,1,512,256]{2,3,1,0:T(8,128)(2,1)}, bf16[4,1,512,256]{2,3,1,0:T(8,128)(2,1)S(1)}, u32[]{:S(2)}) copy-start(bf16[4,1,512,256]{2,3,1,0:T(8,128)(2,1)S(1)} %get-tuple-element.37) | copy-start | bytes 3145732
  66.7 74.6 %all-gather.16.cloned.1.call-start = ((), (), s32[]{:S(2)}) async-start(), calls=%async_computation.11 | async-start | bytes 3145728 | tf_op jit(solution)/shard_map/all_gather | solution.py:94
  67.5 125.0 %all-gather.14.cloned.1.call-start = ((), (), s32[]{:S(2)}) async-start(), calls=%async_computation.5 | async-start | bytes 2359296 | tf_op jit(solution)/shard_map/all_gather | solution.py:74
  68.0 280.8 %all-reduce.10.cloned.1.call-start = ((), (), s32[]{:S(2)}) async-start(), calls=%async_computation.3 | async-start | bytes 16777216 | tf_op jit(solution)/shard_map/psum | solution.py:115
  155.7 47.4 %copy-start.12 = (bf16[4,4,64,512]{3,2,1,0:T(8,128)(2,1)}, bf16[4,4,64,512]{3,2,1,0:T(8,128)(2,1)S(1)}, u32[]{:S(2)}) copy-start(bf16[4,4,64,512]{3,2,1,0:T(8,128)(2,1)S(1)} %fusion.55) | copy-start | bytes 3145732
  160.5 239.6 %all-gather.12.cloned.1.call-start = ((), (), s32[]{:S(2)}) async-start(), calls=%async_computation.4 | async-start | bytes 2359296 | tf_op jit(solution)/shard_map/all_gather | solution.py:73
  161.1 423.2 %all-reduce.14.cloned.1.call-start = ((), (), s32[]{:S(2)}) async-start(), calls=%async_computation.7 | async-start | bytes 16777216 | tf_op jit(solution)/shard_map/psum | solution.py:179
  161.4 41.7 %copy-start.55 = (f32[1,1024]{1,0:T(1,128)}, f32[1,1024]{1,0:T(1,128)S(1)}, u32[]{:S(2)}) copy-start(f32[1,1024]{1,0:T(1,128)S(1)} %get-tuple-element.41) | copy-start | bytes 12292
  161.4 187.5 %copy-start.57 = (f32[1,1024]{1,0:T(1,128)}, f32[1,1024]{1,0:T(1,128)S(1)}, u32[]{:S(2)}) copy-start(f32[1,1024]{1,0:T(1,128)S(1)} %get-tuple-element.42) | copy-start | bytes 12292
  163.8 39.3 %copy-start.26 = (bf16[4,16,1024]{2,0,1:T(4,128)(2,1)}, bf16[4,16,1024]{2,0,1:T(4,128)(2,1)S(1)}, u32[]{:S(2)}) copy-start(bf16[4,16,1024]{2,0,1:T(4,128)(2,1)S(1)} %get-tuple-element.39) | copy-start | bytes 393220
  167.2 245.4 %copy-start.42 = (bf16[4,512,16]{1,2,0:T(8,128)(2,1)}, bf16[4,512,16]{1,2,0:T(8,128)(2,1)S(1)}, u32[]{:S(2)}) copy-start(bf16[4,512,16]{1,2,0:T(8,128)(2,1)S(1)} %fusion.59) | copy-start | bytes 196612
  218.9 136.4 %copy-start.24 = (bf16[4,512,16]{1,2,0:T(8,128)(2,1)}, bf16[4,512,16]{1,2,0:T(8,128)(2,1)S(1)}, u32[]{:S(2)}) copy-start(bf16[4,512,16]{1,2,0:T(8,128)(2,1)S(1)} %all-reduce.19) | copy-start | bytes 196612
  430.7 305.3 %reduce-scatter.5.cloned.1.call-start = ((), (), s32[]{:S(2)}) async-start(), calls=%async_computation.9 | async-start | bytes 6291456 | tf_op jit(solution)/shard_map/reduce_scatter | solution.py:241
  449.9 142.6 %copy-start.58 = (f32[1,1024]{1,0:T(1,128)S(1)}, f32[1,1024]{1,0:T(1,128)}, u32[]{:S(2)}) copy-start(f32[1,1024]{1,0:T(1,128)} %copy-done.57) | copy-start | bytes 12292
  624.5 122.7 %reduce-scatter.3.cloned.1.call-start = ((), (), s32[]{:S(2)}) async-start(), calls=%async_computation.8 | async-start | bytes 6291456 | tf_op jit(solution)/shard_map/reduce_scatter | solution.py:238
  647.7 28.5 %copy-start.15 = (bf16[4,1,512,256]{2,3,1,0:T(8,128)(2,1)S(1)}, bf16[4,1,512,256]{2,3,1,0:T(8,128)(2,1)}, u32[]{:S(2)}) copy-start(bf16[4,1,512,256]{2,3,1,0:T(8,128)(2,1)} %copy-done.14) | copy-start | bytes 3145732
  692.6 88.9 %all-reduce.12.cloned.1.call-start = ((), (), s32[]{:S(2)}) async-start(), calls=%async_computation.6 | async-start | bytes 131072 | tf_op jit(solution)/shard_map/psum | solution.py:139
  723.2 220.7 %all-reduce.16.cloned.1.call-start = ((), (), s32[]{:S(2)}) async-start(), calls=%async_computation.10 | async-start | bytes 16777216 | tf_op jit(solution)/shard_map/psum | solution.py:257
  757.5 27.1 %copy-start.25 = (bf16[4,512,16]{1,2,0:T(8,128)(2,1)S(1)}, bf16[4,512,16]{1,2,0:T(8,128)(2,1)}, u32[]{:S(2)}) copy-start(bf16[4,512,16]{1,2,0:T(8,128)(2,1)} %copy-done.24) | copy-start | bytes 196612
  757.5 360.9 %all-reduce.18.cloned.1.call-start = ((), (), s32[]{:S(2)}) async-start(), calls=%async_computation.14 | async-start | bytes 9437184 | tf_op jit(solution)/shard_map/psum | solution.py:272
  759.7 27.8 %copy-start.13 = (bf16[4,4,64,512]{3,2,1,0:T(8,128)(2,1)S(1)}, bf16[4,4,64,512]{3,2,1,0:T(8,128)(2,1)}, u32[]{:S(2)}) copy-start(bf16[4,4,64,512]{3,2,1,0:T(8,128)(2,1)} %copy-done.12) | copy-start | bytes 3145732
  787.5 25.8 %copy-start.32 = (f32[4,512]{1,0:T(4,128)S(1)}, f32[4,512]{1,0:T(4,128)}, u32[]{:S(2)}) copy-start(f32[4,512]{1,0:T(4,128)} %copy-done.31) | copy-start | bytes 24580
  822.5 121.3 %copy-start.20 = (bf16[4,3,1024,16]{2,0,3,1:T(4,128)(2,1)S(1)}, bf16[4,3,1024,16]{2,0,3,1:T(4,128)(2,1)}, u32[]{:S(2)}) copy-start(bf16[4,3,1024,16]{2,0,3,1:T(4,128)(2,1)} %copy-done.19) | copy-start | bytes 1179652
  822.5 402.3 %all-gather.20.cloned.1.call-start = ((), (), s32[]{:S(2)}) async-start(), calls=%async_computation.13 | async-start | bytes 20971520 | tf_op jit(solution)/shard_map/all_gather | solution.py:137
  831.2 119.1 %copy-start.44 = (f32[4,512]{1,0:T(4,128)S(1)}, f32[4,512]{1,0:T(4,128)}, u32[]{:S(2)}) copy-start(f32[4,512]{1,0:T(4,128)} %copy-done.43) | copy-start | bytes 24580
  831.2 119.1 %copy-start.46 = (f32[4,512]{1,0:T(4,128)S(1)}, f32[4,512]{1,0:T(4,128)}, u32[]{:S(2)}) copy-start(f32[4,512]{1,0:T(4,128)} %copy-done.45) | copy-start | bytes 24580
  (47 other events, 345.0 us)
Sparse Core Ops, SparseCore 0:
  10.7 47.1 all-gather.9
  66.8 39.6 all-gather.17
  108.7 32.5 all-gather.15
  143.3 49.0 all-gather.13
  195.3 153.5 all-reduce.9
  350.9 49.2 all-gather.11
  430.8 153.4 all-reduce.13
  624.7 54.5 reduce-scatter.4
  692.7 54.4 reduce-scatter.2
  750.0 31.5 all-reduce.11
  784.6 159.2 all-reduce.15
  948.5 169.8 all-reduce.17
  1120.0 104.8 all-gather.19
